TPU v7x, 256 devices: a whole 4x4x8 slice. The times are simulated.
256 devices in a mesh: xy: 32 (over z, x_lo, core), gz: 8 (over y, x_hi).
Axes of the slice: x: 4 (x_hi: 2, x_lo: 2; x = x_hi * 2 + x_lo), y: 4, z: 8, core: 2. Of those that a mesh axis runs over, the one named last changes fastest.
Arguments:
- file_data: float32 [512, 64, 8192], P('gz', None, 'xy')
- factor: float32 [512, 256], P('gz'), may hold values from -0.25 to 0.25
- block_owner: int32 [64], replicated, may hold values from 0 to 31, as said below
- block_offset: int32 [64], replicated, may hold values from 0 to 128, as said below
Outputs:
- gram: float32 [512, 512], P('gz')
- core: float32 [256, 64, 8192], P('gz', None, 'xy')
Inputs may be any that keep to these rules, and one draw needn't show every extreme that they name: `block_owner`: block b of device d (b = d * 2 + j) is owned by d - 1, d or d + 1 modulo 32. Every index of xy owns exactly 2 blocks. `block_offset`: offsets are multiples of 128; the blocks of one owner take distinct offsets, so every file slot is named once.
All inputs are finite; a program needn't handle non-finite values.
Results may differ from a plain program's by a relative error of at most 0.00007.
Values sent between devices are 32-bit elements; how exact they have to be, the bound alone decides.
A program may use at most 128 MiB of HBM per device.

v0:
```python
import jax
import jax.numpy as jnp
from jax import lax
from jax.sharding import PartitionSpec as P

BLOCKS_DEV = 2


def shifted(array, axis, by):
    length = lax.axis_size(axis)
    return lax.ppermute(array, axis, [(i, (i + by) % length) for i in range(length)])


def split_up(array, dim, length):
    shape = array.shape
    tiles = array.reshape(*shape[:dim], length, shape[dim] // length, *shape[dim + 1 :])
    return jnp.moveaxis(tiles, dim, 0)


def sent_and_summed(array, axis, dim):
    length = lax.axis_size(axis)
    tiles = lax.all_to_all(split_up(array, dim, length), axis, 0, 0, tiled=True)
    return jnp.sum(tiles, axis=0)


def over_pieces(array, axis):
    tiles = lax.all_gather(array, axis)
    return tiles.sum(axis=0)


def sent_to_all(array, axis):
    length = lax.axis_size(axis)
    return lax.all_to_all(
        jnp.broadcast_to(array[None], (length, *array.shape)), axis, 0, 0, tiled=True
    )


def joined_along(tiles, dim):
    tiles = jnp.moveaxis(tiles, 0, dim)
    shape = tiles.shape
    return tiles.reshape(*shape[:dim], shape[dim] * shape[dim + 1], *shape[dim + 2 :])


def gather_directly(array, axis, dim):
    tiles = sent_to_all(array, axis)
    return joined_along(tiles, dim)


def take_block(buffer, offset):
    return lax.dynamic_slice_in_dim(buffer, offset, 128, 2)


def rebalance(buffer, block_owner, block_offset):
    devices = lax.axis_size("xy")
    myself = lax.axis_index("xy")
    lower_peer = (myself + devices - 1) % devices
    upper_peer = (myself + 1) % devices
    blank = jnp.zeros(buffer.shape[:2] + (128,), buffer.dtype)

    def outgoing(target):
        pieces = []
        for j in range(BLOCKS_DEV):
            owner = block_owner[target * BLOCKS_DEV + j]
            offset = block_offset[target * BLOCKS_DEV + j]
            pieces.append(jnp.where(owner == myself, take_block(buffer, offset), blank))
        return jnp.concatenate(pieces, axis=2)

    from_lower = shifted(outgoing(upper_peer), "xy", 1)
    from_upper = shifted(outgoing(lower_peer), "xy", -1)
    blocks = []
    for j in range(BLOCKS_DEV):
        owner = block_owner[myself * BLOCKS_DEV + j]
        offset = block_offset[myself * BLOCKS_DEV + j]
        local_block = take_block(buffer, offset)
        lower_block = from_lower[:, :, j * 128 : (j + 1) * 128]
        upper_block = from_upper[:, :, j * 128 : (j + 1) * 128]
        remote = jnp.where(owner == lower_peer, lower_block, upper_block)
        blocks.append(jnp.where(owner == myself, local_block, remote))
    return jnp.concatenate(blocks, axis=2)


def used_slots(file_data, block_owner, block_offset):
    myself = lax.axis_index("xy")
    slot_count = file_data.shape[2] // 128
    hits = (block_owner[:, None] == myself) & (
        block_offset[:, None] // 128 == jnp.arange(slot_count, dtype=jnp.int32)[None, :]
    )
    used = jnp.any(hits, axis=0).astype(jnp.float32)
    return jnp.repeat(used, 128)


def local(file_data, factor, block_owner, block_offset):
    working = file_data * used_slots(file_data, block_owner, block_offset)[None, None, :]
    swapped = lax.all_to_all(working, "gz", split_axis=1, concat_axis=0, tiled=True)
    scale = 1.0 / (BLOCKS_DEV * 128 * lax.axis_size("xy") * file_data.shape[1])
    partial_gram = (
        jnp.einsum("zcs,wcs->zw", swapped, swapped, precision=lax.Precision.HIGHEST) * scale
    )
    gram_block = sent_and_summed(partial_gram, "gz", 0)
    gram = over_pieces(gram_block, "xy")
    whole_factor = gather_directly(factor, "gz", 0)
    core_part = jnp.einsum("zr,zcs->rcs", whole_factor, swapped, precision=lax.Precision.HIGHEST)
    core = lax.all_to_all(core_part, "gz", split_axis=0, concat_axis=1, tiled=True)
    core = rebalance(core, block_owner, block_offset)
    return (gram, core)


def solution(mesh):
    return jax.shard_map(
        local,
        mesh=mesh,
        in_specs=(P("gz", None, "xy"), P("gz", None), P(), P()),
        out_specs=(P("gz", None), P("gz", None, "xy")),
        check_vma=False,
    )
```

profile of v0, /device:TPU:1, one launch (start us, length us, event | category | flops | bytes accessed | tf_op | source)
XLA Modules:
  0.0 235.7 jit_solution(13166197315982324203)
XLA Ops:
  7.2 0.0 all-gather.3.cloned.1.call-start
  7.2 0.7 and_select_fusion
  7.9 0.7 broadcast_compare_fusion
  8.5 0.1 and_reduce_fusion
  8.7 0.1 broadcast_bitcast_fusion
  8.7 4.6 %copy_multiply_fusion = f32[64,64,256]{2,0,1:T(8,128)S(1)} fusion(f32[64,64,256]{2,1,0:T(8,128)} %param.4, f32[256]{0:T(256)S(1)} %broadcast_bitcast_fusion), kind=kLoop, calls=%fused_computation.2 | loop fusion | flops 1048576 | bytes 8389632 | tf_op jit(solution)/shard_map/mul | solution.py:93
  13.4 57.3 %all_to_all.46 = f32[64,64,256]{2,0,1:T(8,128)S(1)} all-to-all(f32[64,64,256]{2,0,1:T(8,128)S(1)} %copy_multiply_fusion), channel_id=1, replica_groups=mesh['xy'=32,'gz'=8] {'gz'}, dimensions={1} | all-to-all | bytes 8388608 | tf_op jit(solution)/shard_map/all_to_all | solution.py:94
  70.7 0.0 copy-start
  70.7 0.5 copy.19
  71.2 1.5 copy-done
  72.7 6.9 %fusion.5 = f32[512,512]{1,0:T(8,128)S(1)} fusion(f32[512,8,256]{2,0,1:T(8,128)S(1)} %bitcast.44), kind=kOutput, calls=%fused_computation.9 | convolution fusion | flops 6442713088 | bytes 5242880 | tf_op jit(solution)/shard_map/zcs,wcs->zw/dot_general | solution.py:97
  79.6 0.0 copy-start.2
  79.6 18.5 %all_to_all.47 = f32[8,64,512]{2,1,0:T(8,128)S(1)} all-to-all(f32[8,64,512]{2,1,0:T(8,128)S(1)} %bitcast.50), channel_id=1, replica_groups=mesh['xy'=32,'gz'=8] {'gz'}, dimensions={0} | all-to-all | bytes 2097152 | tf_op jit(solution)/shard_map/all_to_all | solution.py:22
  98.1 0.7 reduce_sum.18
  98.8 0.0 all-gather.3.cloned.1.call-update
  98.8 0.0 copy-done.2
  98.9 11.5 %all_to_all.48 = f32[8,64,256]{2,1,0:T(8,128)S(1)} all-to-all(f32[8,64,256]{2,1,0:T(8,128)S(1)} %broadcast_in_dim.7), channel_id=1, replica_groups=mesh['xy'=32,'gz'=8] {'gz'}, dimensions={0} | all-to-all | bytes 1048576 | tf_op jit(solution)/shard_map/all_to_all | solution.py:33
  110.3 8.6 %fusion.2 = f32[256,8,256]{0,2,1:T(8,128)S(1)} fusion(f32[8,64,256]{2,1,0:T(8,128)S(1)} %all_to_all.48, f32[64,8,8,256]{3,0,2,1:T(8,128)} %bitcast.48), kind=kOutput, calls=%fused_computation.7 | convolution fusion | flops 3221225472 | bytes 6815744 | tf_op jit(solution)/shard_map/zr,zcs->rcs/dot_general | solution.py:102
  118.9 2.0 copy.20
  120.9 0.0 copy-start.3
  120.9 0.0 copy-start.4
  120.9 3.7 %all-to-all-start.3 = ((f32[256,8,256]{2,1,0:T(8,128)}), f32[256,8,256]{2,1,0:T(8,128)S(1)}, u32[]{:S(2)}, u32[]{:S(2)}) async-start(f32[256,8,256]{2,1,0:T(8,128)} %copy.20), calls=%async_computation.3 | async-start | bytes 4194304 | tf_op jit(solution)/shard_map/all_to_all | solution.py:103
  124.7 0.0 copy-done.3
  124.7 0.0 copy-done.4
  124.7 0.7 fusion.10
  135.7 29.0 %all-to-all-done.3 = f32[256,8,256]{2,1,0:T(8,128)S(1)} async-done(((f32[256,8,256]{2,1,0:T(8,128)}), f32[256,8,256]{2,1,0:T(8,128)S(1)}, u32[]{:S(2)}, u32[]{:S(2)}) %all-to-all-start.3) | async-done | bytes 2097184 | tf_op jit(solution)/shard_map/all_to_all | solution.py:103
  164.7 0.0 copy-start.1
  164.7 1.3 copy-done.1
  166.0 1.9 copy.31
  167.9 1.2 dynamic-slice_select_fusion.3
  169.1 1.5 pad_maximum_fusion.1
  170.5 3.9 %collective-permute-start.1 = (f32[32,64,256]{2,1,0:T(8,128)}, f32[32,64,256]{2,1,0:T(8,128)}, u32[]{:S(2)}, u32[]{:S(2)}) collective-permute-start(f32[32,64,256]{2,1,0:T(8,128)} %pad_maximum_fusion.1), channel_id=1, source_target_pairs={{0,248},{8,0},{16,8},{24,16},{32,24},{40,32},{48,40},{56,48},{64,5... | collective-permute-start | bytes 6291464 | tf_op jit(solution)/shard_map/ppermute | solution.py:11
  174.5 1.5 pad_maximum_fusion
  176.0 0.3 collective-permute-start
  182.3 38.9 %collective-permute-done.1 = f32[32,64,256]{2,1,0:T(8,128)} collective-permute-done((f32[32,64,256]{2,1,0:T(8,128)}, f32[32,64,256]{2,1,0:T(8,128)}, u32[]{:S(2)}, u32[]{:S(2)}) %collective-permute-start.1) | collective-permute-done | bytes 2097184 | tf_op jit(solution)/shard_map/ppermute | solution.py:11
  221.3 0.0 collective-permute-done
  221.3 2.9 %fusion.7 = (f32[32,64,128]{2,1,0:T(8,128)S(1)}, f32[32,64,128]{2,1,0:T(8,128)S(1)}) fusion(f32[32,64,256]{2,1,0:T(8,128)} %collective-permute-done.1, f32[32,64,256]{2,1,0:T(8,128)} %collective-permute-done, f32[32,64,256]{2,1,0:T(8,128)S(1)} %bitcast.46, s32[]{:T(128)S(6)} %select_n.112, pred[]{:T(512)S(6)} %eq.53, pred[]{:T(512)S(6)} %eq.52, pred[]{:T(512)S(6)} %eq.59, ...), kind=kLoop, calls=%fused_computation.13 | loop fusion | flops 1048576 | bytes 8388620 | tf_op jit(solution)/shard_map/jit(_where)/select_n | solution.py:78
  224.2 1.5 pad_maximum_fusion.2
  225.7 0.0 all-gather.3.cloned.1.call-done
  225.7 3.2 %reduce_sum.19 = f32[64,512]{1,0:T(8,128)} reduce(f32[32,64,512]{2,1,0:T(8,128)} %bitcast.51, f32[]{:T(128)} %constant.52.clone.1), dimensions={0}, to_apply=%region_2.3 | reduce | flops 1015808 | bytes 4325380 | tf_op jit(solution)/shard_map/reduce_sum | solution.py:28
  (2 shorter events, 0.0 us)
Async XLA Ops:
  7.2 218.5 %all-gather.3.cloned.1.call-start = ((), (), s32[]{:S(2)}) async-start(), calls=%async_computation.4 | async-start | bytes 4325376 | tf_op jit(solution)/shard_map/all_gather | solution.py:27
  70.7 2.0 copy-start
  79.6 19.2 %copy-start.2 = (f32[64,256]{1,0:T(8,128)S(1)}, f32[64,256]{1,0:T(8,128)}, u32[]{:S(2)}) copy-start(f32[64,256]{1,0:T(8,128)} %param.5) | copy-start | bytes 196612
  120.9 3.8 %copy-start.3 = (s32[64]{0:T(128)S(1)}, s32[64]{0:T(128)}, u32[]{:S(2)}) copy-start(s32[64]{0:T(128)} %param.6) | copy-start | bytes 772
  120.9 3.8 %copy-start.4 = (s32[64]{0:T(128)S(1)}, s32[64]{0:T(128)}, u32[]{:S(2)}) copy-start(s32[64]{0:T(128)} %param.7) | copy-start | bytes 772
  120.9 43.8 %all-to-all-start.3 = ((f32[256,8,256]{2,1,0:T(8,128)}), f32[256,8,256]{2,1,0:T(8,128)S(1)}, u32[]{:S(2)}, u32[]{:S(2)}) async-start(f32[256,8,256]{2,1,0:T(8,128)} %copy.20), calls=%async_computation.3 | async-start | bytes 4194304 | tf_op jit(solution)/shard_map/all_to_all | solution.py:103
  164.7 1.3 copy-start.1
  170.5 50.7 %collective-permute-start.1 = (f32[32,64,256]{2,1,0:T(8,128)}, f32[32,64,256]{2,1,0:T(8,128)}, u32[]{:S(2)}, u32[]{:S(2)}) collective-permute-start(f32[32,64,256]{2,1,0:T(8,128)} %pad_maximum_fusion.1), channel_id=1, source_target_pairs={{0,248},{8,0},{16,8},{24,16},{32,24},{40,32},{48,40},{56,48},{64,5... | collective-permute-start | bytes 6291464 | tf_op jit(solution)/shard_map/ppermute | solution.py:11
  176.0 45.3 %collective-permute-start = (f32[32,64,256]{2,1,0:T(8,128)}, f32[32,64,256]{2,1,0:T(8,128)}, u32[]{:S(2)}, u32[]{:S(2)}) collective-permute-start(f32[32,64,256]{2,1,0:T(8,128)} %pad_maximum_fusion), channel_id=1, source_target_pairs={{0,8},{8,16},{16,24},{24,32},{32,40},{40,48},{48,56},{56,64},{64,7... | collective-permute-start | bytes 6291464 | tf_op jit(solution)/shard_map/ppermute | solution.py:11
Sparse Core Ops, SparseCore 0:
  98.9 67.6 all-gather.2
where the time goes:
time: 236 us
  blocking collectives  87.3 us (37%)
  waiting for transfers between devices  68 us (29%)
  between operations  30.5 us (13%)
  other arithmetic  18.6 us (8%)
  matrix products  15.5 us (7%)
  starting transfers between devices  8 us (3%)
  local copies, waits for them, and re-layouts  7.97 us (3%)
    all_to_all x1, blocking collectives, local(): lax.all_to_all(working, 'gz', split_axis=1, concat_axis=0, tiled=True)  57.3 us
    ppermute x2, waiting for transfers between devices, shifted(): lax.ppermute(array, axis, [(i, (i + by) % length) for i in range(length)])  38.9 us
    all_to_all x1, waiting for transfers between devices, local(): lax.all_to_all(core_part, 'gz', split_axis=0, concat_axis=1, tiled=True)  29 us
    all_to_all x1, blocking collectives, sent_and_summed(): tiles = lax.all_to_all(split_up(array, dim, length), axis, 0, 0, tiled=True)  18.5 us
    all_to_all x1, blocking collectives, sent_to_all(): lax.all_to_all(jnp.broadcast_to(array[None], (length, *array.shape)), axi...  11.5 us
    dot_general x1, matrix products, local(): jnp.einsum('zr,zcs->rcs', whole_factor, swapped, precision=lax.Precision....  8.57 us
    dot_general x1, matrix products, local(): jnp.einsum('zcs,wcs->zw', swapped, swapped, precision=lax.Precision.HIGHEST)  6.89 us
  transfers between devices with their start and end apart: 4, of which 2 were waited for; matrix products, arithmetic and copies ran while one was open for 9% of the time, Pallas kernels for 0%

commit v1 on v0

--- a/solution.py
+++ b/solution.py
@@ -4,6 +4,12 @@
 from jax.sharding import PartitionSpec as P
 
 BLOCKS_DEV = 2
+
+
+def exchange_blocks(x, axis, split, join):
+    pieces = jnp.split(x, lax.axis_size(axis), axis=split)
+    incoming = lax.all_to_all(jnp.stack(pieces), axis, 0, 0)
+    return jnp.concatenate(incoming, axis=join)
 
 
 def shifted(array, axis, by):
@@ -91,7 +97,7 @@
 
 def local(file_data, factor, block_owner, block_offset):
     working = file_data * used_slots(file_data, block_owner, block_offset)[None, None, :]
-    swapped = lax.all_to_all(working, "gz", split_axis=1, concat_axis=0, tiled=True)
+    swapped = exchange_blocks(working, "gz", 1, 0)
     scale = 1.0 / (BLOCKS_DEV * 128 * lax.axis_size("xy") * file_data.shape[1])
     partial_gram = (
         jnp.einsum("zcs,wcs->zw", swapped, swapped, precision=lax.Precision.HIGHEST) * scale

time: 236 us -> 236 us (level)
  no operation moved by 1% of the time
where the time goes in v1:
time: 236 us
  blocking collectives  87.1 us (37%)
  waiting for transfers between devices  67.9 us (29%)
  between operations  30.6 us (13%)
  other arithmetic  18.6 us (8%)
  matrix products  15.5 us (7%)
  local copies, waits for them, and re-layouts  8.26 us (4%)
  starting transfers between devices  7.86 us (3%)
    all_to_all x1, blocking collectives, exchange_blocks(): incoming = lax.all_to_all(jnp.stack(pieces), axis, 0, 0)  57.3 us
    ppermute x2, waiting for transfers between devices, shifted(): lax.ppermute(array, axis, [(i, (i + by) % length) for i in range(length)])  38.9 us
    all_to_all x1, waiting for transfers between devices, local(): lax.all_to_all(core_part, 'gz', split_axis=0, concat_axis=1, tiled=True)  29 us
    all_to_all x1, blocking collectives, sent_and_summed(): tiles = lax.all_to_all(split_up(array, dim, length), axis, 0, 0, tiled=True)  18.4 us
    all_to_all x1, blocking collectives, sent_to_all(): lax.all_to_all(jnp.broadcast_to(array[None], (length, *array.shape)), axi...  11.5 us
    dot_general x1, matrix products, local(): jnp.einsum('zr,zcs->rcs', whole_factor, swapped, precision=lax.Precision....  8.57 us
    dot_general x1, matrix products, local(): jnp.einsum('zcs,wcs->zw', swapped, swapped, precision=lax.Precision.HIGHEST)  6.89 us
  transfers between devices with their start and end apart: 4, of which 2 were waited for; matrix products, arithmetic and copies ran while one was open for 9% of the time, Pallas kernels for 0%

profile of v1, /device:TPU:1, one launch (start us, length us, event | category | flops | bytes accessed | tf_op | source)
XLA Modules:
  0.0 235.8 jit_solution(8690321319621518419)
XLA Ops:
  7.2 0.0 all-gather.3.cloned.1.call-start
  7.2 0.7 and_select_fusion
  7.9 0.7 broadcast_compare_fusion
  8.5 0.1 and_reduce_fusion
  8.7 0.1 broadcast_bitcast_fusion
  8.7 4.6 %copy_multiply_fusion = f32[64,64,256]{2,0,1:T(8,128)S(1)} fusion(f32[64,64,256]{2,1,0:T(8,128)} %param.4, f32[256]{0:T(256)S(1)} %broadcast_bitcast_fusion), kind=kLoop, calls=%fused_computation | loop fusion | flops 1048576 | bytes 8389632 | tf_op jit(solution)/shard_map/mul | solution.py:99
  13.7 57.3 %all_to_all.33 = f32[8,64,8,256]{3,1,2,0:T(8,128)S(1)} all-to-all(f32[8,64,8,256]{3,1,2,0:T(8,128)S(1)} %fusion.3), channel_id=1, replica_groups=mesh['xy'=32,'gz'=8] {'gz'}, dimensions={0} | all-to-all | bytes 8388608 | tf_op jit(solution)/shard_map/all_to_all | solution.py:11
  71.0 0.0 copy-start
  71.0 0.5 copy.40
  71.5 1.5 copy-done
  73.0 0.0 copy-start.2
  73.0 6.9 %fusion = f32[512,512]{1,0:T(8,128)S(1)} fusion(f32[512,8,256]{2,0,1:T(8,128)S(1)} %bitcast.71), kind=kOutput, calls=%fused_computation.7 | convolution fusion | flops 6442713088 | bytes 5242880 | tf_op jit(solution)/shard_map/zcs,wcs->zw/dot_general | solution.py:103
  79.9 18.4 %all_to_all.34 = f32[8,64,512]{2,1,0:T(8,128)S(1)} all-to-all(f32[8,64,512]{2,1,0:T(8,128)S(1)} %bitcast.75), channel_id=1, replica_groups=mesh['xy'=32,'gz'=8] {'gz'}, dimensions={0} | all-to-all | bytes 2097152 | tf_op jit(solution)/shard_map/all_to_all | solution.py:28
  98.3 0.7 reduce_sum.18
  99.0 0.0 all-gather.3.cloned.1.call-update
  99.0 0.0 copy-done.2
  99.1 11.5 %all_to_all.35 = f32[8,64,256]{2,1,0:T(8,128)S(1)} all-to-all(f32[8,64,256]{2,1,0:T(8,128)S(1)} %broadcast_in_dim.7), channel_id=1, replica_groups=mesh['xy'=32,'gz'=8] {'gz'}, dimensions={0} | all-to-all | bytes 1048576 | tf_op jit(solution)/shard_map/all_to_all | solution.py:39
  110.6 8.6 %convolution_bitcast_fusion = f32[256,8,256]{0,2,1:T(8,128)S(1)} fusion(f32[8,64,8,256]{3,1,2,0:T(8,128)} %copy-done, f32[8,64,256]{2,1,0:T(8,128)S(1)} %all_to_all.35), kind=kOutput, calls=%fused_computation.5 | convolution fusion | flops 3221225472 | bytes 6815744 | tf_op jit(solution)/shard_map/zr,zcs->rcs/dot_general | solution.py:108
  119.1 0.0 copy-start.3
  119.2 0.0 copy-start.4
  119.2 2.0 copy.41
  121.1 3.6 %all-to-all-start.3 = ((f32[256,8,256]{2,1,0:T(8,128)}), f32[256,8,256]{2,1,0:T(8,128)S(1)}, u32[]{:S(2)}, u32[]{:S(2)}) async-start(f32[256,8,256]{2,1,0:T(8,128)} %copy.41), calls=%async_computation.3 | async-start | bytes 4194304 | tf_op jit(solution)/shard_map/all_to_all | solution.py:109
  124.8 0.0 copy-done.3
  124.8 0.0 copy-done.4
  124.8 0.7 fusion.12
  135.8 29.0 %all-to-all-done.3 = f32[256,8,256]{2,1,0:T(8,128)S(1)} async-done(((f32[256,8,256]{2,1,0:T(8,128)}), f32[256,8,256]{2,1,0:T(8,128)S(1)}, u32[]{:S(2)}, u32[]{:S(2)}) %all-to-all-start.3) | async-done | bytes 2097184 | tf_op jit(solution)/shard_map/all_to_all | solution.py:109
  164.8 0.0 copy-start.1
  164.8 1.3 copy-done.1
  166.1 1.9 copy.46
  167.9 1.2 dynamic-slice_select_fusion.3
  169.1 1.5 pad_maximum_fusion.1
  170.6 3.9 %collective-permute-start.1 = (f32[32,64,256]{2,1,0:T(8,128)}, f32[32,64,256]{2,1,0:T(8,128)}, u32[]{:S(2)}, u32[]{:S(2)}) collective-permute-start(f32[32,64,256]{2,1,0:T(8,128)} %pad_maximum_fusion.1), channel_id=1, source_target_pairs={{0,248},{8,0},{16,8},{24,16},{32,24},{40,32},{48,40},{56,48},{64,5... | collective-permute-start | bytes 6291464 | tf_op jit(solution)/shard_map/ppermute | solution.py:17
  174.5 1.5 pad_maximum_fusion
  176.0 0.3 collective-permute-start
  182.4 38.9 %collective-permute-done.1 = f32[32,64,256]{2,1,0:T(8,128)} collective-permute-done((f32[32,64,256]{2,1,0:T(8,128)}, f32[32,64,256]{2,1,0:T(8,128)}, u32[]{:S(2)}, u32[]{:S(2)}) %collective-permute-start.1) | collective-permute-done | bytes 2097184 | tf_op jit(solution)/shard_map/ppermute | solution.py:17
  221.3 0.0 collective-permute-done
  221.3 2.9 %fusion.2 = (f32[32,64,128]{2,1,0:T(8,128)S(1)}, f32[32,64,128]{2,1,0:T(8,128)S(1)}) fusion(f32[32,64,256]{2,1,0:T(8,128)} %collective-permute-done.1, f32[32,64,256]{2,1,0:T(8,128)} %collective-permute-done, f32[32,64,256]{2,1,0:T(8,128)S(1)} %bitcast.73, s32[]{:T(128)S(6)} %select_n.112, pred[]{:T(512)S(6)} %eq.53, pred[]{:T(512)S(6)} %eq.52, pred[]{:T(512)S(6)} %eq.59, ...), kind=kLoop, calls=%fused_computation.11 | loop fusion | flops 1048576 | bytes 8388620 | tf_op jit(solution)/shard_map/jit(_where)/select_n | solution.py:84
  224.2 1.5 pad_maximum_fusion.2
  225.7 0.0 all-gather.3.cloned.1.call-done
  225.7 3.2 %reduce_sum.19 = f32[64,512]{1,0:T(8,128)} reduce(f32[32,64,512]{2,1,0:T(8,128)} %bitcast.76, f32[]{:T(128)} %constant.52.clone.1), dimensions={0}, to_apply=%region_2.3 | reduce | flops 1015808 | bytes 4325380 | tf_op jit(solution)/shard_map/reduce_sum | solution.py:34
  (10 shorter events, 0.3 us)
Async XLA Ops:
  7.2 218.6 %all-gather.3.cloned.1.call-start = ((), (), s32[]{:S(2)}) async-start(), calls=%async_computation.4 | async-start | bytes 4325376 | tf_op jit(solution)/shard_map/all_gather | solution.py:33
  71.0 2.0 copy-start
  73.0 26.0 %copy-start.2 = (f32[64,256]{1,0:T(8,128)S(1)}, f32[64,256]{1,0:T(8,128)}, u32[]{:S(2)}) copy-start(f32[64,256]{1,0:T(8,128)} %param.5) | copy-start | bytes 196612
  119.1 5.7 %copy-start.3 = (s32[64]{0:T(128)S(1)}, s32[64]{0:T(128)}, u32[]{:S(2)}) copy-start(s32[64]{0:T(128)} %param.6) | copy-start | bytes 772
  119.2 5.6 %copy-start.4 = (s32[64]{0:T(128)S(1)}, s32[64]{0:T(128)}, u32[]{:S(2)}) copy-start(s32[64]{0:T(128)} %param.7) | copy-start | bytes 772
  121.1 43.6 %all-to-all-start.3 = ((f32[256,8,256]{2,1,0:T(8,128)}), f32[256,8,256]{2,1,0:T(8,128)S(1)}, u32[]{:S(2)}, u32[]{:S(2)}) async-start(f32[256,8,256]{2,1,0:T(8,128)} %copy.41), calls=%async_computation.3 | async-start | bytes 4194304 | tf_op jit(solution)/shard_map/all_to_all | solution.py:109
  164.8 1.3 copy-start.1
  170.6 50.7 %collective-permute-start.1 = (f32[32,64,256]{2,1,0:T(8,128)}, f32[32,64,256]{2,1,0:T(8,128)}, u32[]{:S(2)}, u32[]{:S(2)}) collective-permute-start(f32[32,64,256]{2,1,0:T(8,128)} %pad_maximum_fusion.1), channel_id=1, source_target_pairs={{0,248},{8,0},{16,8},{24,16},{32,24},{40,32},{48,40},{56,48},{64,5... | collective-permute-start | bytes 6291464 | tf_op jit(solution)/shard_map/ppermute | solution.py:17
  176.0 45.3 %collective-permute-start = (f32[32,64,256]{2,1,0:T(8,128)}, f32[32,64,256]{2,1,0:T(8,128)}, u32[]{:S(2)}, u32[]{:S(2)}) collective-permute-start(f32[32,64,256]{2,1,0:T(8,128)} %pad_maximum_fusion), channel_id=1, source_target_pairs={{0,8},{8,16},{16,24},{24,32},{32,40},{40,48},{48,56},{56,64},{64,7... | collective-permute-start | bytes 6291464 | tf_op jit(solution)/shard_map/ppermute | solution.py:17
Sparse Core Ops, SparseCore 0:
  99.2 67.4 all-gather.2
